TPU v7x, 32 devices: a whole 2x2x4 slice. The times are simulated.
32 devices in a mesh: row: 8 (over z, x), col: 4 (over y, core).
Axes of the slice: x: 2, y: 2, z: 4, core: 2. Of those that a mesh axis runs over, the one named last changes fastest.
Arguments:
- features: bfloat16 [32768, 1024], P(('row', 'col')), may hold values from -12 to 12
- cotangent: bfloat16 [32768, 1024], P(('row', 'col')), may hold values from -6 to 6
- loader: int32 [32768], replicated, may hold values from 0 to 32767, as said below
- w_query: bfloat16 [1024, 1024], replicated, may hold values from -2 to 2
- w_key: bfloat16 [1024, 1024], replicated, may hold values from -2 to 2
- w_value: bfloat16 [1024, 1024], replicated, may hold values from -0.1875 to 0.1875
- norm_gain: float32 [1024], replicated, may hold values from 0.25 to 1.75
- send_blocks: int32 [32, 4, 2], replicated, may hold values from -1 to 7, as said below
- tile_lists: int32 [256, 3], P(('row', 'col')), may hold values from 0 to 15, as said below
Outputs:
- layer_out: bfloat16 [32768, 1024], P(('row', 'col'))
- grad_features: bfloat16 [32768, 1024], P(('row', 'col'))
Inputs may be any that keep to these rules, and one draw needn't show every extreme that they name: `loader`: a permutation of the 32768 node numbers; the 1024 rows of each device hold exactly 32 nodes owned by each device. `send_blocks`: entry [e, p, s] is a block of device e (a number below 8) sent to the device of e's row group with col index p in slot s, or -1 for an empty slot; the nonempty slots of one (e, p) come first and name distinct blocks; slots toward e's own col index are empty; all 2 slots toward the next col index (cyclically) are filled. `tile_lists`: row b names 3 distinct entries of the tile table of b's device, never b's own block and never an empty slot; every nonempty received slot is named by some block of its device.
All inputs are finite; a program needn't handle non-finite values.
Results may differ from a plain program's by a relative error of at most 0.012.
The roundings to bfloat16 on the way count: a program that leaves them out, or rounds other values in their place, can miss the bound.
Values may be sent and summed in bfloat16 or wider, within the bound.
No kernel may reach another device: no remote copies, remote signals or barrier semaphores. Data moves between devices by JAX's collectives and lax.ppermute only.
A program may use at most 256 MiB of HBM per device.

v0:
```python
import jax
import jax.numpy as jnp
from jax import lax
from jax.sharding import PartitionSpec as P

HEADS = 8
HEAD_DIM = 128


def attend(queries, key_rows, value_rows, cot_rows, gain_row):
    count = queries.shape[0]
    width = queries.shape[2]
    q_heads = queries.reshape(count, -1, HEADS, HEAD_DIM)
    k_heads = key_rows.reshape(count, -1, HEADS, HEAD_DIM)
    v_heads = value_rows.reshape(count, -1, HEADS, HEAD_DIM)
    score_scale = HEAD_DIM ** (-0.5)
    scores = (
        jnp.einsum("bqhd,bkhd->bhqk", q_heads, k_heads, preferred_element_type=jnp.float32)
        * score_scale
    )
    row_max = jnp.max(scores, axis=-1, keepdims=True)
    expo = jnp.exp(scores - row_max)
    prob_full = expo / jnp.sum(expo, axis=-1, keepdims=True)
    prob_half = prob_full.astype(jnp.bfloat16)
    mixed_out = jnp.einsum(
        "bhqk,bkhd->bqhd", prob_half, v_heads, preferred_element_type=jnp.float32
    ).reshape(count, -1, width)
    inv_rms = lax.rsqrt(jnp.mean(mixed_out * mixed_out, axis=-1, keepdims=True) + 1e-06)
    normed = (mixed_out * inv_rms * gain_row).astype(jnp.bfloat16)
    grad_in = cot_rows.astype(jnp.float32) * gain_row
    inner = jnp.mean(grad_in * mixed_out, axis=-1, keepdims=True)
    grad_mix = (inv_rms * (grad_in - mixed_out * inv_rms * inv_rms * inner)).astype(jnp.bfloat16)
    grad_heads = grad_mix.reshape(count, -1, HEADS, HEAD_DIM)
    grad_prob = jnp.einsum(
        "bqhd,bkhd->bhqk", grad_heads, v_heads, preferred_element_type=jnp.float32
    )
    delta = jnp.sum(prob_full * grad_prob, axis=-1, keepdims=True)
    grad_score = (prob_full * (grad_prob - delta) * score_scale).astype(jnp.bfloat16)
    grad_query = jnp.einsum(
        "bhqk,bkhd->bqhd", grad_score, k_heads, preferred_element_type=jnp.float32
    )
    grad_query = grad_query.reshape(count, -1, width).astype(jnp.bfloat16)
    grad_key = jnp.einsum(
        "bhqk,bqhd->bkhd", grad_score, q_heads, preferred_element_type=jnp.float32
    ).reshape(count, -1, width)
    grad_value = jnp.einsum(
        "bhqk,bqhd->bkhd", prob_half, grad_heads, preferred_element_type=jnp.float32
    ).reshape(count, -1, width)
    return (normed, grad_query, grad_key, grad_value)


def project_back(kv_rows, w_key, w_value, width):
    contract = (((1,), (1,)), ((), ()))
    total = lax.dot_general(kv_rows[:, :width], w_key, contract, preferred_element_type=jnp.float32)
    return total + lax.dot_general(
        kv_rows[:, width:], w_value, contract, preferred_element_type=jnp.float32
    )


def body(features, cotangent, loader, w_query, w_key, w_value, norm_gain, send_blocks, tile_lists):
    row_count = lax.axis_size("row")
    col_count = lax.axis_size("col")
    devices = row_count * col_count
    self_index = lax.axis_index("row") * col_count + lax.axis_index("col")
    rows_dev = features.shape[0]
    width = features.shape[1]
    per_peer = rows_dev // devices
    block_count = tile_lists.shape[0]
    block_rows = rows_dev // block_count
    capacity = send_blocks.shape[2]
    slots = block_count + col_count * capacity
    my_nodes = lax.dynamic_slice_in_dim(loader, self_index * rows_dev, rows_dev)
    send_order = jnp.argsort(my_nodes // rows_dev, stable=True)
    back_order = jnp.argsort(send_order)
    all_owners = (loader // rows_dev).reshape(devices, rows_dev)
    arrive_pos = jnp.argsort(jnp.where(all_owners == self_index, 0, 1), axis=1, stable=True)[
        :, :per_peer
    ]
    arriving = (
        jnp.take_along_axis(loader.reshape(devices, rows_dev), arrive_pos, axis=1).reshape(rows_dev)
        - self_index * rows_dev
    )
    placing = jnp.argsort(arriving)

    def regroup(buffer):
        return lax.all_to_all(buffer, ("row", "col"), split_axis=0, concat_axis=0, tiled=True)

    outgoing = jnp.concatenate([features[send_order], cotangent[send_order]], axis=1).reshape(
        devices, per_peer, 2 * width
    )
    incoming = regroup(outgoing).reshape(rows_dev, 2 * width)[placing]
    owned_rows = incoming[:, :width]
    owned_cot = incoming[:, width:]
    queries = jnp.dot(owned_rows, w_query, preferred_element_type=jnp.float32).astype(jnp.bfloat16)
    key_all = jnp.dot(owned_rows, w_key, preferred_element_type=jnp.float32).astype(jnp.bfloat16)
    value_all = jnp.dot(owned_rows, w_value, preferred_element_type=jnp.float32).astype(
        jnp.bfloat16
    )
    kv_local = jnp.concatenate([key_all, value_all], axis=1).reshape(
        block_count, block_rows, 2 * width
    )
    send_row = lax.dynamic_index_in_dim(send_blocks, self_index, 0, keepdims=False)
    filled = (send_row >= 0)[:, :, None, None]
    picked = jnp.maximum(send_row, 0)
    outbound = jnp.where(filled, kv_local[picked], jnp.zeros((), jnp.bfloat16))
    arrived_kv = lax.all_to_all(outbound, "col", split_axis=0, concat_axis=0, tiled=True).reshape(
        col_count * capacity, block_rows, 2 * width
    )
    tile_table = jnp.concatenate([kv_local, arrived_kv], axis=0)
    read_entries = jnp.concatenate(
        [jnp.arange(block_count, dtype=jnp.int32)[:, None], tile_lists], axis=1
    )
    group_size = 4
    group_count = block_count // group_size

    def per_group(totals, inputs):
        q_group, cot_group, read_group = inputs
        picked_kv = tile_table[read_group].reshape(group_size, -1, 2 * width)
        normed, grad_query, grad_key, grad_value = attend(
            q_group, picked_kv[:, :, :width], picked_kv[:, :, width:], cot_group, norm_gain
        )
        grad_tiles = jnp.concatenate(
            [grad_key.reshape(-1, block_rows, width), grad_value.reshape(-1, block_rows, width)],
            axis=2,
        )
        totals = totals.at[read_group.reshape(-1)].add(grad_tiles)
        return (totals, (normed, grad_query))

    group_inputs = (
        queries.reshape(group_count, group_size, block_rows, width),
        owned_cot.reshape(group_count, group_size, block_rows, width),
        read_entries.reshape(group_count, group_size, -1),
    )
    start = jnp.zeros((slots, block_rows, 2 * width), jnp.float32)
    entry_grads, (normed_all, grad_query_all) = lax.scan(per_group, start, group_inputs)
    remote_kv = entry_grads[block_count:].astype(jnp.bfloat16)
    back_hot = (
        send_row[:, :, None] == jnp.arange(block_count, dtype=jnp.int32)[None, None, :]
    ).astype(jnp.float32)
    back_hot = back_hot.reshape(col_count * capacity, block_count)
    remote_rows = remote_kv.reshape(col_count * capacity * block_rows, 2 * width)
    remote_proj = project_back(remote_rows, w_key, w_value, width).astype(jnp.bfloat16)
    remote_proj = remote_proj.reshape(col_count, capacity, block_rows * width)
    returned = lax.all_to_all(remote_proj, "col", split_axis=0, concat_axis=0, tiled=True)
    returned = returned.reshape(col_count * capacity, block_rows * width).astype(jnp.float32)
    back_sum = lax.dot_general(
        back_hot, returned, (((0,), (0,)), ((), ())), precision=lax.Precision.HIGHEST
    )
    local_kv = entry_grads[:block_count].reshape(rows_dev, 2 * width).astype(jnp.bfloat16)
    grad_query_rows = grad_query_all.reshape(rows_dev, width)
    contract = (((1,), (1,)), ((), ()))
    grad_owned = lax.dot_general(
        grad_query_rows, w_query, contract, preferred_element_type=jnp.float32
    )
    grad_owned = grad_owned + project_back(local_kv, w_key, w_value, width)
    grad_owned = (grad_owned + back_sum.reshape(rows_dev, width)).astype(jnp.bfloat16)
    layer_rows = normed_all.reshape(rows_dev, width)
    layer_back = regroup(layer_rows[arriving].reshape(devices, per_peer, width)).reshape(
        rows_dev, width
    )[back_order]
    grad_back = regroup(grad_owned[arriving].reshape(devices, per_peer, width)).reshape(
        rows_dev, width
    )[back_order]
    return (layer_back, grad_back)


def solution(mesh):
    in_specs = (
        P(("row", "col"), None),
        P(("row", "col"), None),
        P(),
        P(),
        P(),
        P(),
        P(),
        P(),
        P(("row", "col"), None),
    )
    out_specs = (P(("row", "col"), None), P(("row", "col"), None))
    return jax.shard_map(body, mesh=mesh, in_specs=in_specs, out_specs=out_specs, check_vma=False)
```

profile of v0, /device:TPU:0, one launch (start us, length us, event | category | flops | bytes accessed | tf_op | source)
XLA Modules:
  0.0 880.2 jit_solution(3138944694689780795)
XLA Ops:
  62.4 72.3 %all-to-all-done = bf16[32,32,2048]{2,1,0:T(8,128)(2,1)} async-done(((bf16[32,32,2048]{2,1,0:T(8,128)(2,1)}), bf16[32,32,2048]{2,1,0:T(8,128)(2,1)}, u32[]{:S(2)}, u32[]{:S(2)}) %all-to-all-start) | async-done | bytes 4194336 | tf_op jit(solution)/shard_map/all_to_all | solution.py:86
  134.7 11.6 %gather_fusion.3 = bf16[1024,2048]{1,0:T(8,128)(2,1)} fusion(bf16[1024,2048]{1,0:T(8,128)(2,1)} %bitcast.16, s32[1024]{0:T(1024)S(1)} %fusion.62), kind=kCustom, calls=%fused_computation.3 | custom fusion | bytes 8392704 | tf_op jit(solution)/shard_map/gather | solution.py:91
  171.2 20.7 %all-to-all-start.1 = ((bf16[4,2,128,2048]{3,2,1,0:T(8,128)(2,1)}), bf16[4,2,128,2048]{3,2,1,0:T(8,128)(2,1)}, u32[]{:S(2)}, u32[]{:S(2)}) async-start(bf16[4,2,128,2048]{3,2,1,0:T(8,128)(2,1)} %broadcast_select_fusion), calls=%async_computation.1 | async-start | bytes 8388608 | tf_op jit(solution)/shard_map/all_to_all | solution.py:106
  200.5 39.6 %all-to-all-done.1 = bf16[4,2,128,2048]{3,2,1,0:T(8,128)(2,1)} async-done(((bf16[4,2,128,2048]{3,2,1,0:T(8,128)(2,1)}), bf16[4,2,128,2048]{3,2,1,0:T(8,128)(2,1)}, u32[]{:S(2)}, u32[]{:S(2)}) %all-to-all-start.1) | async-done | bytes 4194336 | tf_op jit(solution)/shard_map/all_to_all | solution.py:106
  255.3 454.2 %while.14 = (s32[]{:T(128)}, f32[16,128,2048]{2,1,0:T(8,128)}, bf16[2,4,128,1024]{3,2,1,0:T(8,128)(2,1)}, bf16[2,4,128,1024]{3,2,1,0:T(8,128)(2,1)}, s32[2,4,4]{...) while((s32[]{:T(128)}, f32[16,128,2048]{2,1,0:T(8,128)}, ...), condition=%wide.region_10.11_spmd, body=%wide.region_3.10_spmd.sunk | while | flops 3283102720 | bytes 372362752 | solution.py:135
  309.6 35.2 %fusion.127 = bf16[4,8,128,128]{3,2,1,0:T(8,128)(2,1)} fusion(bf16[4,512,8,128]{1,3,2,0:T(8,128)(2,1)} %bitcast.135, f32[4,8,128,512]{3,2,1,0:T(8,128)} %fusion.125, f32[4,8,128,512]{3,2,1,0:T(8,128)} %get-tuple-element.201, f32[4,8,128]{2,1,0:T(8,128)S(1)} %get-tuple-element.202), kind=kOutput, calls=%fused_computation.43.clone.1 | convolution fusion | flops 552079872 | bytes 22036480 | tf_op jit(solution)/shard_map/while/body/eval_jaxpr/bhqk,bkhd->bqhd/dot_general | solution.py:39
  354.2 35.9 %fusion.126 = f32[4,512,8,128]{1,3,2,0:T(8,128)} fusion(bf16[4,128,8,128]{1,3,2,0:T(8,128)(2,1)} %bitcast.140, f32[4,8,128,512]{3,2,1,0:T(8,128)} %fusion.125, f32[4,8,128,512]{3,2,1,0:T(8,128)} %get-tuple-element.201, f32[4,8,128]{2,1,0:T(8,128)S(1)} %get-tuple-element.202), kind=kOutput, calls=%fused_computation.24.clone.1 | convolution fusion | flops 551555584 | bytes 26230784 | tf_op jit(solution)/shard_map/while/body/eval_jaxpr/bhqk,bqhd->bkhd/dot_general | solution.py:43
  390.1 9.9 %copy.103 = f32[4,512,8,128]{3,2,1,0:T(8,128)} copy(f32[4,512,8,128]{1,3,2,0:T(8,128)} %fusion.126) | data formatting | bytes 16777216 | tf_op jit(solution)/shard_map/while/body/eval_jaxpr/bhqk,bqhd->bkhd/transpose | solution.py:43
  400.0 9.3 %reshape.404 = f32[16,128,1024]{2,1,0:T(8,128)} reshape(f32[4,512,8,128]{3,2,1,0:T(8,128)} %copy.103) | data formatting | bytes 16777216 | tf_op jit(solution)/shard_map/while/body/eval_jaxpr/reshape;while/body/eval_jaxpr/reshape | solution.py:123
  417.3 9.9 %copy.102 = f32[4,512,8,128]{3,2,1,0:T(8,128)} copy(f32[4,512,8,128]{1,3,2,0:T(8,128)} %convolution_bitcast_fusion.3) | data formatting | bytes 16777216 | tf_op jit(solution)/shard_map/while/body/eval_jaxpr/bhqk,bqhd->bkhd/transpose | solution.py:46
  427.2 9.2 %reshape.403 = f32[16,128,1024]{2,1,0:T(8,128)} reshape(f32[4,512,8,128]{3,2,1,0:T(8,128)} %copy.102) | data formatting | bytes 16777216 | tf_op jit(solution)/shard_map/while/body/eval_jaxpr/reshape;while/body/eval_jaxpr/reshape | solution.py:123
  436.4 11.7 %pad_maximum_fusion.5 = f32[16,128,2048]{2,1,0:T(8,128)} fusion(f32[16,128,1024]{2,1,0:T(8,128)} %reshape.403, f32[16,128,1024]{2,1,0:T(8,128)} %reshape.404), kind=kLoop, calls=%fused_computation.13.clone.1 | loop fusion | flops 4194304 | bytes 33554432 | tf_op jit(solution)/shard_map/while/body/eval_jaxpr/concatenate | solution.py:122
  448.2 34.2 %scatter_fusion = f32[16,128,2048]{2,1,0:T(8,128)} fusion(f32[16,128,2048]{2,1,0:T(8,128)} %get-tuple-element.219, s32[16]{0:T(128)S(1)} %fusion.120, f32[16,128,2048]{2,1,0:T(8,128)} %pad_maximum_fusion.5), kind=kCustom, calls=%fused_computation.10.clone.1 | custom fusion | flops 4194304 | bytes 50331712 | tf_op jit(solution)/shard_map/while/body/eval_jaxpr/scatter-add | solution.py:126
  536.7 35.2 %fusion.127 = bf16[4,8,128,128]{3,2,1,0:T(8,128)(2,1)} fusion(bf16[4,512,8,128]{1,3,2,0:T(8,128)(2,1)} %bitcast.135, f32[4,8,128,512]{3,2,1,0:T(8,128)} %fusion.125, f32[4,8,128,512]{3,2,1,0:T(8,128)} %get-tuple-element.201, f32[4,8,128]{2,1,0:T(8,128)S(1)} %get-tuple-element.202), kind=kOutput, calls=%fused_computation.43.clone.1 | convolution fusion | flops 552079872 | bytes 22036480 | tf_op jit(solution)/shard_map/while/body/eval_jaxpr/bhqk,bkhd->bqhd/dot_general | solution.py:39
  581.3 35.9 %fusion.126 = f32[4,512,8,128]{1,3,2,0:T(8,128)} fusion(bf16[4,128,8,128]{1,3,2,0:T(8,128)(2,1)} %bitcast.140, f32[4,8,128,512]{3,2,1,0:T(8,128)} %fusion.125, f32[4,8,128,512]{3,2,1,0:T(8,128)} %get-tuple-element.201, f32[4,8,128]{2,1,0:T(8,128)S(1)} %get-tuple-element.202), kind=kOutput, calls=%fused_computation.24.clone.1 | convolution fusion | flops 551555584 | bytes 26230784 | tf_op jit(solution)/shard_map/while/body/eval_jaxpr/bhqk,bqhd->bkhd/dot_general | solution.py:43
  617.2 9.9 %copy.103 = f32[4,512,8,128]{3,2,1,0:T(8,128)} copy(f32[4,512,8,128]{1,3,2,0:T(8,128)} %fusion.126) | data formatting | bytes 16777216 | tf_op jit(solution)/shard_map/while/body/eval_jaxpr/bhqk,bqhd->bkhd/transpose | solution.py:43
  627.1 9.3 %reshape.404 = f32[16,128,1024]{2,1,0:T(8,128)} reshape(f32[4,512,8,128]{3,2,1,0:T(8,128)} %copy.103) | data formatting | bytes 16777216 | tf_op jit(solution)/shard_map/while/body/eval_jaxpr/reshape;while/body/eval_jaxpr/reshape | solution.py:123
  644.4 9.9 %copy.102 = f32[4,512,8,128]{3,2,1,0:T(8,128)} copy(f32[4,512,8,128]{1,3,2,0:T(8,128)} %convolution_bitcast_fusion.3) | data formatting | bytes 16777216 | tf_op jit(solution)/shard_map/while/body/eval_jaxpr/bhqk,bqhd->bkhd/transpose | solution.py:46
  663.5 11.7 %pad_maximum_fusion.5 = f32[16,128,2048]{2,1,0:T(8,128)} fusion(f32[16,128,1024]{2,1,0:T(8,128)} %reshape.403, f32[16,128,1024]{2,1,0:T(8,128)} %reshape.404), kind=kLoop, calls=%fused_computation.13.clone.1 | loop fusion | flops 4194304 | bytes 33554432 | tf_op jit(solution)/shard_map/while/body/eval_jaxpr/concatenate | solution.py:122
  675.3 34.2 %scatter_fusion = f32[16,128,2048]{2,1,0:T(8,128)} fusion(f32[16,128,2048]{2,1,0:T(8,128)} %get-tuple-element.219, s32[16]{0:T(128)S(1)} %fusion.120, f32[16,128,2048]{2,1,0:T(8,128)} %pad_maximum_fusion.5), kind=kCustom, calls=%fused_computation.10.clone.1 | custom fusion | flops 4194304 | bytes 50331712 | tf_op jit(solution)/shard_map/while/body/eval_jaxpr/scatter-add | solution.py:126
  741.7 17.7 %all-to-all-done.3 = bf16[4,2,131072]{2,1,0:T(2,128)(2,1)} async-done(((bf16[4,2,131072]{2,1,0:T(2,128)(2,1)}), bf16[4,2,131072]{2,1,0:T(2,128)(2,1)}, u32[]{:S(2)}, u32[]{:S(2)}) %all-to-all-start.3) | async-done | bytes 2097184 | tf_op jit(solution)/shard_map/all_to_all | solution.py:144
  784.9 9.6 %add_convert_fusion = bf16[1024,1024]{1,0:T(8,128)(2,1)} fusion(f32[1024,1024]{1,0:T(8,128)} %reshape.283, f32[1024,1024]{1,0:T(8,128)} %fusion.48, f32[1024,1024]{1,0:T(8,128)} %fusion.46, bf16[1024,1024]{1,0:T(8,128)(2,1)} %bitcast.159, bf16[1024,1024]{1,0:T(8,128)(2,1)} %param.14), kind=kOutput, calls=%fused_computation.65 | convolution fusion | flops 2151677952 | bytes 18874368 | tf_op jit(solution)/shard_map/dot_general | solution.py:152
  802.3 9.9 %all-to-all-done.2 = bf16[32,32,1024]{2,1,0:T(8,128)(2,1)} async-done(((bf16[32,32,1024]{2,1,0:T(8,128)(2,1)}), bf16[32,32,1024]{2,1,0:T(8,128)(2,1)}, u32[]{:S(2)}, u32[]{:S(2)}) %all-to-all-start.2) | async-done | bytes 2097184 | tf_op jit(solution)/shard_map/all_to_all | solution.py:86
  828.8 36.5 %all-to-all-done.4 = bf16[32,32,1024]{2,1,0:T(8,128)(2,1)} async-done(((bf16[32,32,1024]{2,1,0:T(8,128)(2,1)}), bf16[32,32,1024]{2,1,0:T(8,128)(2,1)}, u32[]{:S(2)}, u32[]{:S(2)}) %all-to-all-start.4) | async-done | bytes 2097184 | tf_op jit(solution)/shard_map/all_to_all | solution.py:86
  (170 shorter events, 346.2 us)
Async XLA Ops:
  7.2 139.1 %copy-start = (bf16[1024,1024]{1,0:T(8,128)(2,1)S(1)}, bf16[1024,1024]{1,0:T(8,128)(2,1)}, u32[]{:S(2)}) copy-start(bf16[1024,1024]{1,0:T(8,128)(2,1)} %param.16) | copy-start | bytes 6291460
  12.4 7.9 copy-start.13
  32.9 7.5 copy-start.9
  32.9 9.0 %copy-start.17 = (s32[32,4,2]{0,2,1:T(2,128)S(1)}, s32[32,4,2]{0,2,1:T(2,128)}, u32[]{:S(2)}) copy-start(s32[32,4,2]{0,2,1:T(2,128)} %param.18) | copy-start | bytes 3076
  32.9 101.8 %all-to-all-start = ((bf16[32,32,2048]{2,1,0:T(8,128)(2,1)}), bf16[32,32,2048]{2,1,0:T(8,128)(2,1)}, u32[]{:S(2)}, u32[]{:S(2)}) async-start(bf16[32,32,2048]{2,1,0:T(8,128)(2,1)} %bitcast.146), calls=%async_computation | async-start | bytes 8388608 | tf_op jit(solution)/shard_map/all_to_all | solution.py:86
  40.3 7.5 sort.70.cloned.1.call-start
  57.9 88.3 %copy-start.11 = (s32[32,32]{1,0:T(8,128)}, s32[32,32]{1,0:T(8,128)S(1)}, u32[]{:S(2)}) copy-start(s32[32,32]{1,0:T(8,128)S(1)} %select_subtract_fusion) | copy-start | bytes 12292
  146.2 4.1 copy-start.6
  146.2 4.2 copy-start.19
  171.1 20.7 %copy-start.18 = (s32[8,3]{0,1:T(4,128)S(1)}, s32[8,3]{0,1:T(4,128)}, u32[]{:S(2)}) copy-start(s32[8,3]{0,1:T(4,128)} %param.19) | copy-start | bytes 292
  171.2 68.9 %all-to-all-start.1 = ((bf16[4,2,128,2048]{3,2,1,0:T(8,128)(2,1)}), bf16[4,2,128,2048]{3,2,1,0:T(8,128)(2,1)}, u32[]{:S(2)}, u32[]{:S(2)}) async-start(bf16[4,2,128,2048]{3,2,1,0:T(8,128)(2,1)} %broadcast_select_fusion), calls=%async_computation.1 | async-start | bytes 8388608 | tf_op jit(solution)/shard_map/all_to_all | solution.py:106
  247.5 7.8 copy-start.10
  295.5 7.9 copy-start.3
  400.0 9.3 %copy-start.5 = (bf16[4,128,8,128]{1,3,2,0:T(8,128)(2,1)S(1)}, bf16[4,128,8,128]{1,3,2,0:T(8,128)(2,1)}, u32[]{:S(2)}) copy-start(bf16[4,128,8,128]{1,3,2,0:T(8,128)(2,1)} %copy-done.4) | copy-start | bytes 3145732 | tf_op jit(solution)/shard_map/while
  522.6 7.9 copy-start.3
  627.1 9.3 %copy-start.5 = (bf16[4,128,8,128]{1,3,2,0:T(8,128)(2,1)S(1)}, bf16[4,128,8,128]{1,3,2,0:T(8,128)(2,1)}, u32[]{:S(2)}) copy-start(bf16[4,128,8,128]{1,3,2,0:T(8,128)(2,1)} %copy-done.4) | copy-start | bytes 3145732 | tf_op jit(solution)/shard_map/while
  724.7 9.0 %copy-start.12 = (s32[32,32]{1,0:T(8,128)S(1)}, s32[32,32]{1,0:T(8,128)}, u32[]{:S(2)}) copy-start(s32[32,32]{1,0:T(8,128)} %copy-done.11) | copy-start | bytes 12292
  729.2 30.3 %all-to-all-start.3 = ((bf16[4,2,131072]{2,1,0:T(2,128)(2,1)}), bf16[4,2,131072]{2,1,0:T(2,128)(2,1)}, u32[]{:S(2)}, u32[]{:S(2)}) async-start(bf16[4,2,131072]{2,1,0:T(2,128)(2,1)} %reshape.282), calls=%async_computation.3 | async-start | bytes 4194304 | tf_op jit(solution)/shard_map/all_to_all | solution.py:144
  759.5 52.8 %all-to-all-start.2 = ((bf16[32,32,1024]{2,1,0:T(8,128)(2,1)}), bf16[32,32,1024]{2,1,0:T(8,128)(2,1)}, u32[]{:S(2)}, u32[]{:S(2)}) async-start(bf16[32,32,1024]{2,1,0:T(8,128)(2,1)} %bitcast.148), calls=%async_computation.2 | async-start | bytes 4194304 | tf_op jit(solution)/shard_map/all_to_all | solution.py:86
  763.5 6.1 copy-start.8
  763.5 6.1 copy-start.21
  769.6 4.3 copy-start.16
  802.3 14.2 %copy-start.14 = (s32[1024]{0:T(1024)S(1)}, s32[1024]{0:T(1024)}, u32[]{:S(2)}) copy-start(s32[1024]{0:T(1024)} %copy-done.13) | copy-start | bytes 12292
  812.3 53.0 %all-to-all-start.4 = ((bf16[32,32,1024]{2,1,0:T(8,128)(2,1)}), bf16[32,32,1024]{2,1,0:T(8,128)(2,1)}, u32[]{:S(2)}, u32[]{:S(2)}) async-start(bf16[32,32,1024]{2,1,0:T(8,128)(2,1)} %bitcast.149), calls=%async_computation.4 | async-start | bytes 4194304 | tf_op jit(solution)/shard_map/all_to_all | solution.py:86
  (9 other events, 17.1 us)
Sparse Core Ops, SparseCore 0:
  44.2 3.2 sort.72.cloned.1.call-done
  (1 shorter events, 0.0 us)
where the time goes:
time: 893 us; the launch traced here: 880 us
  local copies, waits for them, and re-layouts  268 us (30%)
  matrix products  241 us (27%)
  waiting for transfers between devices  176 us (20%)
  other arithmetic  140 us (16%)
  starting transfers between devices  40.9 us (5%)
  between operations  14.5 us (2%)
    all_to_all x3, waiting for transfers between devices, regroup(): lax.all_to_all(buffer, ('row', 'col'), split_axis=0, concat_axis=0, tiled...  119 us
    dot_general x2, matrix products, attend(): jnp.einsum('bhqk,bqhd->bkhd', grad_score, q_heads, preferred_element_type...  71.7 us
    dot_general x2, matrix products, attend(): jnp.einsum('bhqk,bkhd->bqhd', grad_score, k_heads, preferred_element_type...  70.4 us
    scatter-add x2, other arithmetic, per_group(): totals = totals.at[read_group.reshape(-1)].add(grad_tiles)  68.4 us
    all_to_all x1, waiting for transfers between devices, body(): lax.all_to_all(outbound, 'col', split_axis=0, concat_axis=0, tiled=True)  39.6 us
    slice x4, local copies, waits for them, and re-layouts, per_group(): picked_kv[:, :, :width]  24.2 us
    concatenate x2, other arithmetic, per_group(): jnp.concatenate([grad_key.reshape(-1, block_rows, width), grad_value.resh...  23.3 us
    all_to_all x1, starting transfers between devices, body(): lax.all_to_all(outbound, 'col', split_axis=0, concat_axis=0, tiled=True)  20.7 us
  transfers between devices with their start and end apart: 5, of which 5 were waited for; matrix products, arithmetic and copies ran while one was open for 10% of the time, Pallas kernels for 0%

commit v1 on v0

--- a/solution.py
+++ b/solution.py
@@ -5,6 +5,28 @@
 
 HEADS = 8
 HEAD_DIM = 128
+
+
+def in_blocks(x, dim, length):
+    before, after = (x.shape[:dim], x.shape[dim + 1 :])
+    return jnp.moveaxis(x.reshape(*before, length, -1, *after), dim, 0)
+
+
+def laid_out(blocks, dim):
+    blocks = jnp.moveaxis(blocks, 0, dim)
+    lengths = blocks.shape
+    return blocks.reshape(*lengths[:dim], lengths[dim] * lengths[dim + 1], *lengths[dim + 2 :])
+
+
+def swapped_with_each(value, axis, split_dim, concat_dim):
+    size, position = (lax.axis_size(axis), lax.axis_index(axis))
+    parts = in_blocks(value, split_dim, size)
+    outs = [parts[position]]
+    for step in range(1, size):
+        sent = parts[position ^ step]
+        outs.append(lax.ppermute(sent, axis, [(i, i ^ step) for i in range(size)]))
+    parts = jnp.stack(outs)[position ^ jnp.arange(size)]
+    return laid_out(parts, concat_dim)
 
 
 def attend(queries, key_rows, value_rows, cot_rows, gain_row):
@@ -141,7 +163,7 @@
     remote_rows = remote_kv.reshape(col_count * capacity * block_rows, 2 * width)
     remote_proj = project_back(remote_rows, w_key, w_value, width).astype(jnp.bfloat16)
     remote_proj = remote_proj.reshape(col_count, capacity, block_rows * width)
-    returned = lax.all_to_all(remote_proj, "col", split_axis=0, concat_axis=0, tiled=True)
+    returned = swapped_with_each(remote_proj, "col", 0, 0)
     returned = returned.reshape(col_count * capacity, block_rows * width).astype(jnp.float32)
     back_sum = lax.dot_general(
         back_hot, returned, (((0,), (0,)), ((), ())), precision=lax.Precision.HIGHEST

time: 893 us -> 889 us (level)
  local copies, waits for them, and re-layouts: 268 us -> 287 us
  waiting for transfers between devices: 176 us -> 157 us
  starting transfers between devices: 40.9 us -> 26.1 us
  other arithmetic: 140 us -> 151 us
    all_to_all x1 -> x0, waiting for transfers between devices: 17.7 us -> none  [body(): lax.all_to_all(remote_proj, 'col', split_axis=0, concat_axis=0, tiled=True)]
    all_to_all x1, starting transfers between devices: 20.7 us -> 5.13 us  [body(): lax.all_to_all(outbound, 'col', split_axis=0, concat_axis=0, tiled=True)]
    gather x0 -> x3, local copies, waits for them, and re-layouts: none -> 11.2 us  [swapped_with_each(): parts = jnp.stack(outs)[position ^ jnp.arange(size)]]
    ppermute x0 -> x3, waiting for transfers between devices: none -> 10.4 us  [swapped_with_each(): outs.append(lax.ppermute(sent, axis, [(i, i ^ step) for i in range(size)]))]
    all_to_all x3, waiting for transfers between devices: 119 us -> 109 us  [regroup(): lax.all_to_all(buffer, ('row', 'col'), split_axis=0, concat_axis=0, tiled...]
  transfers between devices with their start and end apart: 5 -> 7, of which waited for: 5 -> 4; matrix products, arithmetic and copies ran while one was open for 10% -> 13% of each run, Pallas kernels for 0% -> 0%
where the time goes in v1:
time: 889 us; the launch traced here: 876 us
  local copies, waits for them, and re-layouts  287 us (32%)
  matrix products  240 us (27%)
  waiting for transfers between devices  157 us (18%)
  other arithmetic  151 us (17%)
  starting transfers between devices  26.1 us (3%)
  between operations  14.7 us (2%)
    all_to_all x3, waiting for transfers between devices, regroup(): lax.all_to_all(buffer, ('row', 'col'), split_axis=0, concat_axis=0, tiled...  109 us
    dot_general x2, matrix products, attend(): jnp.einsum('bhqk,bqhd->bkhd', grad_score, q_heads, preferred_element_type...  71.7 us
    dot_general x2, matrix products, attend(): jnp.einsum('bhqk,bkhd->bqhd', grad_score, k_heads, preferred_element_type...  70.4 us
    scatter-add x2, other arithmetic, per_group(): totals = totals.at[read_group.reshape(-1)].add(grad_tiles)  68.4 us
    all_to_all x1, waiting for transfers between devices, body(): lax.all_to_all(outbound, 'col', split_axis=0, concat_axis=0, tiled=True)  37.5 us
    slice x4, local copies, waits for them, and re-layouts, per_group(): picked_kv[:, :, :width]  24.2 us
    concatenate x2, other arithmetic, per_group(): jnp.concatenate([grad_key.reshape(-1, block_rows, width), grad_value.resh...  23.3 us
    transpose x2, local copies, waits for them, and re-layouts, attend(): jnp.einsum('bhqk,bqhd->bkhd', grad_score, q_heads, preferred_element_type...  19.9 us
  transfers between devices with their start and end apart: 7, of which 4 were waited for; matrix products, arithmetic and copies ran while one was open for 13% of the time, Pallas kernels for 0%

profile of v1, /device:TPU:0, one launch (start us, length us, event | category | flops | bytes accessed | tf_op | source)
XLA Modules:
  0.0 876.5 jit_solution(8850724626194814495)
XLA Ops:
  48.5 8.6 gather_fusion.9
  62.4 72.3 %all-to-all-done = bf16[32,32,2048]{2,1,0:T(8,128)(2,1)} async-done(((bf16[32,32,2048]{2,1,0:T(8,128)(2,1)}), bf16[32,32,2048]{2,1,0:T(8,128)(2,1)}, u32[]{:S(2)}, u32[]{:S(2)}) %all-to-all-start) | async-done | bytes 4194336 | tf_op jit(solution)/shard_map/all_to_all | solution.py:108
  134.7 11.6 %gather_fusion.3 = bf16[1024,2048]{1,0:T(8,128)(2,1)} fusion(bf16[1024,2048]{1,0:T(8,128)(2,1)} %bitcast.16, s32[1024]{0:T(1024)S(1)} %fusion.61), kind=kCustom, calls=%fused_computation.3 | custom fusion | bytes 8392704 | tf_op jit(solution)/shard_map/gather | solution.py:113
  187.0 37.5 %all-to-all-done.1 = bf16[4,2,128,2048]{3,2,1,0:T(8,128)(2,1)} async-done(((bf16[4,2,128,2048]{3,2,1,0:T(8,128)(2,1)}), bf16[4,2,128,2048]{3,2,1,0:T(8,128)(2,1)}, u32[]{:S(2)}, u32[]{:S(2)}) %all-to-all-start.1) | async-done | bytes 4194336 | tf_op jit(solution)/shard_map/all_to_all | solution.py:128
  239.8 454.8 %while.14 = (s32[]{:T(128)}, f32[16,128,2048]{2,1,0:T(8,128)}, bf16[2,4,128,1024]{3,2,1,0:T(8,128)(2,1)}, bf16[2,4,128,1024]{3,2,1,0:T(8,128)(2,1)}, s32[2,4,4]{...) while((s32[]{:T(128)}, f32[16,128,2048]{2,1,0:T(8,128)}, ...), condition=%wide.region_10.11_spmd, body=%wide.region_3.10_spmd.sunk | while | flops 3283102720 | bytes 372362752 | solution.py:157
  294.5 35.2 %fusion.129 = bf16[4,8,128,128]{3,2,1,0:T(8,128)(2,1)} fusion(bf16[4,512,8,128]{1,3,2,0:T(8,128)(2,1)} %bitcast.151, f32[4,8,128,512]{3,2,1,0:T(8,128)} %fusion.127, f32[4,8,128,512]{3,2,1,0:T(8,128)} %get-tuple-element.198, f32[4,8,128]{2,1,0:T(8,128)S(1)} %get-tuple-element.199), kind=kOutput, calls=%fused_computation.45.clone.1 | convolution fusion | flops 552079872 | bytes 22036480 | tf_op jit(solution)/shard_map/while/body/eval_jaxpr/bhqk,bkhd->bqhd/dot_general | solution.py:61
  339.1 35.9 %fusion.128 = f32[4,512,8,128]{1,3,2,0:T(8,128)} fusion(bf16[4,128,8,128]{1,3,2,0:T(8,128)(2,1)} %bitcast.156, f32[4,8,128,512]{3,2,1,0:T(8,128)} %fusion.127, f32[4,8,128,512]{3,2,1,0:T(8,128)} %get-tuple-element.198, f32[4,8,128]{2,1,0:T(8,128)S(1)} %get-tuple-element.199), kind=kOutput, calls=%fused_computation.26.clone.1 | convolution fusion | flops 551555584 | bytes 26230784 | tf_op jit(solution)/shard_map/while/body/eval_jaxpr/bhqk,bqhd->bkhd/dot_general | solution.py:65
  375.0 9.9 %copy.74 = f32[4,512,8,128]{3,2,1,0:T(8,128)} copy(f32[4,512,8,128]{1,3,2,0:T(8,128)} %fusion.128) | data formatting | bytes 16777216 | tf_op jit(solution)/shard_map/while/body/eval_jaxpr/bhqk,bqhd->bkhd/transpose | solution.py:65
  384.9 9.3 %reshape.440 = f32[16,128,1024]{2,1,0:T(8,128)} reshape(f32[4,512,8,128]{3,2,1,0:T(8,128)} %copy.74) | data formatting | bytes 16777216 | tf_op jit(solution)/shard_map/while/body/eval_jaxpr/reshape;while/body/eval_jaxpr/reshape | solution.py:145
  402.2 9.9 %copy.73 = f32[4,512,8,128]{3,2,1,0:T(8,128)} copy(f32[4,512,8,128]{1,3,2,0:T(8,128)} %convolution_bitcast_fusion.2) | data formatting | bytes 16777216 | tf_op jit(solution)/shard_map/while/body/eval_jaxpr/bhqk,bqhd->bkhd/transpose | solution.py:68
  412.1 9.2 %reshape.439 = f32[16,128,1024]{2,1,0:T(8,128)} reshape(f32[4,512,8,128]{3,2,1,0:T(8,128)} %copy.73) | data formatting | bytes 16777216 | tf_op jit(solution)/shard_map/while/body/eval_jaxpr/reshape;while/body/eval_jaxpr/reshape | solution.py:145
  421.3 11.7 %pad_maximum_fusion.7 = f32[16,128,2048]{2,1,0:T(8,128)} fusion(f32[16,128,1024]{2,1,0:T(8,128)} %reshape.439, f32[16,128,1024]{2,1,0:T(8,128)} %reshape.440), kind=kLoop, calls=%fused_computation.15.clone.1 | loop fusion | flops 4194304 | bytes 33554432 | tf_op jit(solution)/shard_map/while/body/eval_jaxpr/concatenate | solution.py:144
  433.1 34.2 %scatter_fusion = f32[16,128,2048]{2,1,0:T(8,128)} fusion(f32[16,128,2048]{2,1,0:T(8,128)} %get-tuple-element.216, s32[16]{0:T(128)S(1)} %fusion.122, f32[16,128,2048]{2,1,0:T(8,128)} %pad_maximum_fusion.7), kind=kCustom, calls=%fused_computation.12.clone.1 | custom fusion | flops 4194304 | bytes 50331712 | tf_op jit(solution)/shard_map/while/body/eval_jaxpr/scatter-add | solution.py:148
  521.6 35.2 %fusion.129 = bf16[4,8,128,128]{3,2,1,0:T(8,128)(2,1)} fusion(bf16[4,512,8,128]{1,3,2,0:T(8,128)(2,1)} %bitcast.151, f32[4,8,128,512]{3,2,1,0:T(8,128)} %fusion.127, f32[4,8,128,512]{3,2,1,0:T(8,128)} %get-tuple-element.198, f32[4,8,128]{2,1,0:T(8,128)S(1)} %get-tuple-element.199), kind=kOutput, calls=%fused_computation.45.clone.1 | convolution fusion | flops 552079872 | bytes 22036480 | tf_op jit(solution)/shard_map/while/body/eval_jaxpr/bhqk,bkhd->bqhd/dot_general | solution.py:61
  566.2 35.9 %fusion.128 = f32[4,512,8,128]{1,3,2,0:T(8,128)} fusion(bf16[4,128,8,128]{1,3,2,0:T(8,128)(2,1)} %bitcast.156, f32[4,8,128,512]{3,2,1,0:T(8,128)} %fusion.127, f32[4,8,128,512]{3,2,1,0:T(8,128)} %get-tuple-element.198, f32[4,8,128]{2,1,0:T(8,128)S(1)} %get-tuple-element.199), kind=kOutput, calls=%fused_computation.26.clone.1 | convolution fusion | flops 551555584 | bytes 26230784 | tf_op jit(solution)/shard_map/while/body/eval_jaxpr/bhqk,bqhd->bkhd/dot_general | solution.py:65
  602.1 9.9 %copy.74 = f32[4,512,8,128]{3,2,1,0:T(8,128)} copy(f32[4,512,8,128]{1,3,2,0:T(8,128)} %fusion.128) | data formatting | bytes 16777216 | tf_op jit(solution)/shard_map/while/body/eval_jaxpr/bhqk,bqhd->bkhd/transpose | solution.py:65
  612.1 9.3 %reshape.440 = f32[16,128,1024]{2,1,0:T(8,128)} reshape(f32[4,512,8,128]{3,2,1,0:T(8,128)} %copy.74) | data formatting | bytes 16777216 | tf_op jit(solution)/shard_map/while/body/eval_jaxpr/reshape;while/body/eval_jaxpr/reshape | solution.py:145
  629.3 9.9 %copy.73 = f32[4,512,8,128]{3,2,1,0:T(8,128)} copy(f32[4,512,8,128]{1,3,2,0:T(8,128)} %convolution_bitcast_fusion.2) | data formatting | bytes 16777216 | tf_op jit(solution)/shard_map/while/body/eval_jaxpr/bhqk,bqhd->bkhd/transpose | solution.py:68
  639.2 9.2 %reshape.439 = f32[16,128,1024]{2,1,0:T(8,128)} reshape(f32[4,512,8,128]{3,2,1,0:T(8,128)} %copy.73) | data formatting | bytes 16777216 | tf_op jit(solution)/shard_map/while/body/eval_jaxpr/reshape;while/body/eval_jaxpr/reshape | solution.py:145
  648.5 11.7 %pad_maximum_fusion.7 = f32[16,128,2048]{2,1,0:T(8,128)} fusion(f32[16,128,1024]{2,1,0:T(8,128)} %reshape.439, f32[16,128,1024]{2,1,0:T(8,128)} %reshape.440), kind=kLoop, calls=%fused_computation.15.clone.1 | loop fusion | flops 4194304 | bytes 33554432 | tf_op jit(solution)/shard_map/while/body/eval_jaxpr/concatenate | solution.py:144
  660.2 34.2 %scatter_fusion = f32[16,128,2048]{2,1,0:T(8,128)} fusion(f32[16,128,2048]{2,1,0:T(8,128)} %get-tuple-element.216, s32[16]{0:T(128)S(1)} %fusion.122, f32[16,128,2048]{2,1,0:T(8,128)} %pad_maximum_fusion.7), kind=kCustom, calls=%fused_computation.12.clone.1 | custom fusion | flops 4194304 | bytes 50331712 | tf_op jit(solution)/shard_map/while/body/eval_jaxpr/scatter-add | solution.py:148
  743.0 10.4 %collective-permute-done.2 = bf16[1,2,131072]{2,1,0:T(2,128)(2,1)} collective-permute-done((bf16[1,2,131072]{2,1,0:T(2,128)(2,1)S(1)}, bf16[1,2,131072]{2,1,0:T(2,128)(2,1)}, u32[]{:S(2)}, u32[]{:S(2)}) %collective-permute-start.2) | collective-permute-done | bytes 524320 | tf_op jit(solution)/shard_map/ppermute | solution.py:27
  787.2 9.6 %add_convert_fusion = bf16[1024,1024]{1,0:T(8,128)(2,1)} fusion(f32[1024,1024]{1,0:T(8,128)} %reshape.298, f32[1024,1024]{1,0:T(8,128)} %fusion.48, f32[1024,1024]{1,0:T(8,128)} %fusion.46, bf16[1024,1024]{1,0:T(8,128)(2,1)} %bitcast.176, bf16[1024,1024]{1,0:T(8,128)(2,1)} %param.14), kind=kOutput, calls=%fused_computation.66 | convolution fusion | flops 2151677952 | bytes 18874368 | tf_op jit(solution)/shard_map/dot_general | solution.py:174
  824.9 36.5 %all-to-all-done.3 = bf16[32,32,1024]{2,1,0:T(8,128)(2,1)} async-done(((bf16[32,32,1024]{2,1,0:T(8,128)(2,1)}), bf16[32,32,1024]{2,1,0:T(8,128)(2,1)}, u32[]{:S(2)}, u32[]{:S(2)}) %all-to-all-start.3) | async-done | bytes 2097184 | tf_op jit(solution)/shard_map/all_to_all | solution.py:108
  (176 shorter events, 363.8 us)
Async XLA Ops:
  7.2 139.1 %copy-start = (bf16[1024,1024]{1,0:T(8,128)(2,1)S(1)}, bf16[1024,1024]{1,0:T(8,128)(2,1)}, u32[]{:S(2)}) copy-start(bf16[1024,1024]{1,0:T(8,128)(2,1)} %param.16) | copy-start | bytes 6291460
  12.4 7.9 copy-start.13
  32.9 7.5 copy-start.9
  32.9 9.0 %copy-start.12 = (s32[32,4,2]{0,2,1:T(2,128)S(1)}, s32[32,4,2]{0,2,1:T(2,128)}, u32[]{:S(2)}) copy-start(s32[32,4,2]{0,2,1:T(2,128)} %param.18) | copy-start | bytes 3076
  32.9 101.8 %all-to-all-start = ((bf16[32,32,2048]{2,1,0:T(8,128)(2,1)}), bf16[32,32,2048]{2,1,0:T(8,128)(2,1)}, u32[]{:S(2)}, u32[]{:S(2)}) async-start(bf16[32,32,2048]{2,1,0:T(8,128)(2,1)} %bitcast.162), calls=%async_computation | async-start | bytes 8388608 | tf_op jit(solution)/shard_map/all_to_all | solution.py:108
  40.3 7.4 sort.70.cloned.1.call-start
  146.2 4.1 copy-start.6
  146.2 4.1 copy-start.17
  171.1 5.2 copy-start.16
  171.1 53.4 %all-to-all-start.1 = ((bf16[4,2,128,2048]{3,2,1,0:T(8,128)(2,1)}), bf16[4,2,128,2048]{3,2,1,0:T(8,128)(2,1)}, u32[]{:S(2)}, u32[]{:S(2)}) async-start(bf16[4,2,128,2048]{3,2,1,0:T(8,128)(2,1)} %broadcast_select_fusion), calls=%async_computation.1 | async-start | bytes 8388608 | tf_op jit(solution)/shard_map/all_to_all | solution.py:128
  231.9 7.8 copy-start.10
  280.4 7.9 copy-start.3
  384.9 9.3 %copy-start.5 = (bf16[4,128,8,128]{1,3,2,0:T(8,128)(2,1)S(1)}, bf16[4,128,8,128]{1,3,2,0:T(8,128)(2,1)}, u32[]{:S(2)}) copy-start(bf16[4,128,8,128]{1,3,2,0:T(8,128)(2,1)} %copy-done.4) | copy-start | bytes 3145732 | tf_op jit(solution)/shard_map/while
  507.6 7.9 copy-start.3
  612.1 9.3 %copy-start.5 = (bf16[4,128,8,128]{1,3,2,0:T(8,128)(2,1)S(1)}, bf16[4,128,8,128]{1,3,2,0:T(8,128)(2,1)}, u32[]{:S(2)}) copy-start(bf16[4,128,8,128]{1,3,2,0:T(8,128)(2,1)} %copy-done.4) | copy-start | bytes 3145732 | tf_op jit(solution)/shard_map/while
  714.3 6.0 copy-start.8
  718.4 24.5 %collective-permute-start = (bf16[1,2,131072]{2,1,0:T(2,128)(2,1)}, bf16[1,2,131072]{2,1,0:T(2,128)(2,1)}, u32[]{:S(2)}, u32[]{:S(2)}) collective-permute-start(bf16[1,2,131072]{2,1,0:T(2,128)(2,1)} %get-tuple-element.127), channel_id=1, source_target_pairs={{0,1},{1,0},{2,3},{3,2},{4,5},{5,4},{6,7},{7,6},{8,9},{9,8},{10,11... | collective-permute-start | bytes 1572872 | tf_op jit(solution)/shard_map/ppermute | solution.py:27
  718.4 24.5 %collective-permute-start.1 = (bf16[1,2,131072]{2,1,0:T(2,128)(2,1)}, bf16[1,2,131072]{2,1,0:T(2,128)(2,1)}, u32[]{:S(2)}, u32[]{:S(2)}) collective-permute-start(bf16[1,2,131072]{2,1,0:T(2,128)(2,1)} %get-tuple-element.126), channel_id=1, source_target_pairs={{0,2},{1,3},{2,0},{3,1},{4,6},{5,7},{6,4},{7,5},{8,10},{9,11},{10,... | collective-permute-start | bytes 1572872 | tf_op jit(solution)/shard_map/ppermute | solution.py:27
  719.0 34.4 %collective-permute-start.2 = (bf16[1,2,131072]{2,1,0:T(2,128)(2,1)S(1)}, bf16[1,2,131072]{2,1,0:T(2,128)(2,1)}, u32[]{:S(2)}, u32[]{:S(2)}) collective-permute-start(bf16[1,2,131072]{2,1,0:T(2,128)(2,1)S(1)} %get-tuple-element.125), channel_id=1, source_target_pairs={{0,3},{1,2},{2,1},{3,0},{4,7},{5,6},{6,5},{7,4},{8,11},{9,10},{10,... | collective-permute-start | bytes 1572872 | tf_op jit(solution)/shard_map/ppermute | solution.py:27
  720.3 4.4 copy-start.11
  732.6 72.2 %all-to-all-start.2 = ((bf16[32,32,1024]{2,1,0:T(8,128)(2,1)}), bf16[32,32,1024]{2,1,0:T(8,128)(2,1)}, u32[]{:S(2)}, u32[]{:S(2)}) async-start(bf16[32,32,1024]{2,1,0:T(8,128)(2,1)} %bitcast.164), calls=%async_computation.2 | async-start | bytes 4194304 | tf_op jit(solution)/shard_map/all_to_all | solution.py:108
  769.5 8.4 copy-start.15
  804.7 7.9 copy-start.14
  804.7 56.6 %all-to-all-start.3 = ((bf16[32,32,1024]{2,1,0:T(8,128)(2,1)}), bf16[32,32,1024]{2,1,0:T(8,128)(2,1)}, u32[]{:S(2)}, u32[]{:S(2)}) async-start(bf16[32,32,1024]{2,1,0:T(8,128)(2,1)} %bitcast.165), calls=%async_computation.3 | async-start | bytes 4194304 | tf_op jit(solution)/shard_map/all_to_all | solution.py:108
  (8 other events, 17.2 us)
Sparse Core Ops, SparseCore 0:
  44.2 3.2 sort.72.cloned.1.call-done
  (1 shorter events, 0.0 us)
